TPU v7x, 256 devices: a whole 4x4x8 slice. The times are simulated.
256 devices in a mesh: clique: 8 (over y_hi, x), copy: 32 (over z, y_lo, core).
Axes of the slice: x: 4, y: 4 (y_hi: 2, y_lo: 2; y = y_hi * 2 + y_lo), z: 8, core: 2. Of those that a mesh axis runs over, the one named last changes fastest.
Arguments:
- out_grad: bfloat16 [524288, 512], P(('clique', 'copy')), may hold values from -6 to 6
- pre_act: bfloat16 [524288, 512], P(('clique', 'copy')), may hold values from -6 to 6
- batch_count: int32 [256], P(('clique', 'copy')), may hold values from 1024 to 2048, as said below
- layer_two: bfloat16 [512, 512], replicated, may hold values from -0.25 to 0.25
- hot_slots: int32 [524288, 10], P(('clique', 'copy')), may hold values from 0 to 4095
- cold_index: int32 [524288, 15], P(('clique', 'copy')), may hold values from 0 to 2047
- hot_feats: bfloat16 [4096, 768], P('clique'), may hold values from -6 to 6
- cold_feats: bfloat16 [524288, 768], P(('clique', 'copy')), may hold values from -6 to 6
Outputs:
- grad_one: float32 [768, 512], replicated
- grad_two: float32 [512, 512], replicated
Inputs may be any that keep to these rules, and one draw needn't show every extreme that they name: `batch_count`: some device has all 2048 rows live in every draw.
All inputs are finite; a program needn't handle non-finite values.
Results may differ from a plain program's by a relative error of at most 0.015.
Values may be sent and summed in bfloat16 or wider, within the bound.
A program may use at most 128 MiB of HBM per device.

v0:
```python
import jax
import jax.numpy as jnp
from jax import lax
from jax.sharding import PartitionSpec as P


def table_sums(index_cols, row_grad, table_rows, fanout):
    block = min(512, table_rows)
    blocks = table_rows // block
    offsets = jnp.arange(block, dtype=jnp.int32)

    def one_block(start):
        wanted = start + offsets
        counts = jnp.zeros((block, index_cols.shape[0]), jnp.float32)
        for column in range(index_cols.shape[1]):
            counts = counts + (index_cols[:, column][None, :] == wanted[:, None]).astype(
                jnp.float32
            )
        summed = jnp.dot(counts.astype(jnp.bfloat16), row_grad, preferred_element_type=jnp.float32)
        return (summed * (1.0 / fanout)).astype(jnp.bfloat16)

    starts = jnp.arange(blocks, dtype=jnp.int32) * block
    parts = lax.map(one_block, starts)
    return parts.reshape(table_rows, row_grad.shape[1])


def on_device(
    out_grad, pre_act, batch_count, layer_two, hot_slots, cold_index, hot_feats, cold_feats
):
    rows = out_grad.shape[0]
    hot_local = hot_feats.shape[0]
    hot_total = hot_local * lax.axis_size("clique")
    k_hot = hot_slots.shape[1]
    k_cold = cold_index.shape[1]
    fanout = k_hot + k_cold
    cold_rows = cold_feats.shape[0]
    live = (jnp.arange(rows, dtype=jnp.int32) < batch_count[0])[:, None]
    masked = jnp.where(live, out_grad, jnp.zeros_like(out_grad))
    activ = jnp.maximum(pre_act, jnp.zeros_like(pre_act))
    grad_two = jnp.dot(activ.T, masked, preferred_element_type=jnp.float32)
    back = jnp.dot(masked, layer_two.T, preferred_element_type=jnp.float32)
    row_grad = jnp.where(pre_act > 0, back, jnp.zeros_like(back)).astype(jnp.bfloat16)
    hot_part = table_sums(hot_slots, row_grad, hot_total, fanout)
    summed = lax.psum(hot_part, "clique").astype(jnp.float32)
    owned = lax.dynamic_slice_in_dim(summed, lax.axis_index("clique") * hot_local, hot_local, 0)
    cold_part = table_sums(cold_index, row_grad, cold_rows, fanout)
    grad_one = jnp.dot(cold_feats.T, cold_part, preferred_element_type=jnp.float32)
    grad_one = grad_one + jnp.dot(
        hot_feats.T, owned.astype(jnp.bfloat16), preferred_element_type=jnp.float32
    )
    total_one, total_two = lax.psum((grad_one, grad_two), ("clique", "copy"))
    return (total_one, total_two)


def solution(mesh):
    placed = (
        P(("clique", "copy"), None),
        P(("clique", "copy"), None),
        P(("clique", "copy")),
        P(),
        P(("clique", "copy"), None),
        P(("clique", "copy"), None),
        P("clique", None),
        P(("clique", "copy"), None),
    )
    return jax.shard_map(
        on_device, mesh=mesh, in_specs=placed, out_specs=(P(), P()), check_vma=False
    )
```

profile of v0, /device:TPU:2, one launch (start us, length us, event | category | flops | bytes accessed | tf_op | source)
XLA Modules:
  0.0 475.0 jit_solution(12058573302038147682)
XLA Ops:
  7.2 0.0 copy-start
  7.2 0.0 all-reduce.4.cloned.1.call-start
  8.1 5.2 %select_convert_fusion = bf16[2048,512]{1,0:T(8,128)(2,1)} fusion(bf16[2048,512]{1,0:T(8,128)(2,1)} %param.13, bf16[512,512]{1,0:T(8,128)(2,1)} %param.15, bf16[2048,512]{1,0:T(8,128)(2,1)} %param.12, pred[2048]{0:T(1024)(128)(4,1)S(1)} %iota_compare_fusion), kind=kOutput, calls=%fused_computation.43 | convolution fusion | flops 1077936128 | bytes 6817792 | tf_op jit(solution)/shard_map/dot_general | solution.py:41
  13.2 63.4 %while.23 = (s32[]{:T(128)}, bf16[8,512,512]{2,1,0:T(8,128)(2,1)}, s32[2048,10]{0,1:T(8,128)S(1)}, s32[8]{0:T(128)S(1)}, bf16[2048,512]{1,0:T(8,128)(2,1)}, /*index=5*/s32[]{:T(128)}) while((s32[]{:T(128)}, bf16[8,512,512]{2,1,0:T(8,128)(2,1)}, s32[2048,10]{0,1:T(8,128)S(1)}, s32[8]{0:T(128)S(1)}, bf16[2048,512]{1,0:T(8,128)(2,1)}, ...), condition=%wide.region_3.4_spmd.clone, body=%wide.region_2.3_spmd.clone.sunk | while | flops 1105723904 | bytes 2871893 | solution.py:23
  13.2 0.1 fusion.67
  13.3 0.6 dynamic_slice.22
  13.9 0.6 iota_add_fusion.5
  14.6 6.6 %fusion.68 = bf16[8,512,512]{2,1,0:T(8,128)(2,1)} fusion(bf16[8,512,512]{2,1,0:T(8,128)(2,1)} %get-tuple-element.278, s32[]{:T(128)} %get-tuple-element.277, bf16[2048,512]{1,0:T(8,128)(2,1)} %get-tuple-element.287, s32[2048]{0:T(1024)S(1)} %bitcast.126, s32[2048]{0:T(1024)S(1)} %bitcast.127, s32[2048]{0:T(1024)S(1)} %bitcast.128, ...), kind=kOutput, calls=%fused_computation.41.clone.1 | convolution fusion | flops 1105723392 | bytes 2705920 | tf_op jit(solution)/shard_map/while/body/eval_jaxpr/dot_general | solution.py:19
  21.2 0.1 fusion.67
  21.2 0.6 dynamic_slice.22
  21.9 0.6 iota_add_fusion.5
  22.5 6.6 %fusion.68 = bf16[8,512,512]{2,1,0:T(8,128)(2,1)} fusion(bf16[8,512,512]{2,1,0:T(8,128)(2,1)} %get-tuple-element.278, s32[]{:T(128)} %get-tuple-element.277, bf16[2048,512]{1,0:T(8,128)(2,1)} %get-tuple-element.287, s32[2048]{0:T(1024)S(1)} %bitcast.126, s32[2048]{0:T(1024)S(1)} %bitcast.127, s32[2048]{0:T(1024)S(1)} %bitcast.128, ...), kind=kOutput, calls=%fused_computation.41.clone.1 | convolution fusion | flops 1105723392 | bytes 2705920 | tf_op jit(solution)/shard_map/while/body/eval_jaxpr/dot_general | solution.py:19
  29.1 0.1 fusion.67
  29.2 0.6 dynamic_slice.22
  29.8 0.6 iota_add_fusion.5
  30.4 6.6 %fusion.68 = bf16[8,512,512]{2,1,0:T(8,128)(2,1)} fusion(bf16[8,512,512]{2,1,0:T(8,128)(2,1)} %get-tuple-element.278, s32[]{:T(128)} %get-tuple-element.277, bf16[2048,512]{1,0:T(8,128)(2,1)} %get-tuple-element.287, s32[2048]{0:T(1024)S(1)} %bitcast.126, s32[2048]{0:T(1024)S(1)} %bitcast.127, s32[2048]{0:T(1024)S(1)} %bitcast.128, ...), kind=kOutput, calls=%fused_computation.41.clone.1 | convolution fusion | flops 1105723392 | bytes 2705920 | tf_op jit(solution)/shard_map/while/body/eval_jaxpr/dot_general | solution.py:19
  37.0 0.1 fusion.67
  37.1 0.6 dynamic_slice.22
  37.7 0.6 iota_add_fusion.5
  38.4 6.6 %fusion.68 = bf16[8,512,512]{2,1,0:T(8,128)(2,1)} fusion(bf16[8,512,512]{2,1,0:T(8,128)(2,1)} %get-tuple-element.278, s32[]{:T(128)} %get-tuple-element.277, bf16[2048,512]{1,0:T(8,128)(2,1)} %get-tuple-element.287, s32[2048]{0:T(1024)S(1)} %bitcast.126, s32[2048]{0:T(1024)S(1)} %bitcast.127, s32[2048]{0:T(1024)S(1)} %bitcast.128, ...), kind=kOutput, calls=%fused_computation.41.clone.1 | convolution fusion | flops 1105723392 | bytes 2705920 | tf_op jit(solution)/shard_map/while/body/eval_jaxpr/dot_general | solution.py:19
  44.9 0.1 fusion.67
  45.0 0.6 dynamic_slice.22
  45.6 0.6 iota_add_fusion.5
  46.3 6.6 %fusion.68 = bf16[8,512,512]{2,1,0:T(8,128)(2,1)} fusion(bf16[8,512,512]{2,1,0:T(8,128)(2,1)} %get-tuple-element.278, s32[]{:T(128)} %get-tuple-element.277, bf16[2048,512]{1,0:T(8,128)(2,1)} %get-tuple-element.287, s32[2048]{0:T(1024)S(1)} %bitcast.126, s32[2048]{0:T(1024)S(1)} %bitcast.127, s32[2048]{0:T(1024)S(1)} %bitcast.128, ...), kind=kOutput, calls=%fused_computation.41.clone.1 | convolution fusion | flops 1105723392 | bytes 2705920 | tf_op jit(solution)/shard_map/while/body/eval_jaxpr/dot_general | solution.py:19
  52.9 0.1 fusion.67
  52.9 0.6 dynamic_slice.22
  53.6 0.6 iota_add_fusion.5
  54.2 6.6 %fusion.68 = bf16[8,512,512]{2,1,0:T(8,128)(2,1)} fusion(bf16[8,512,512]{2,1,0:T(8,128)(2,1)} %get-tuple-element.278, s32[]{:T(128)} %get-tuple-element.277, bf16[2048,512]{1,0:T(8,128)(2,1)} %get-tuple-element.287, s32[2048]{0:T(1024)S(1)} %bitcast.126, s32[2048]{0:T(1024)S(1)} %bitcast.127, s32[2048]{0:T(1024)S(1)} %bitcast.128, ...), kind=kOutput, calls=%fused_computation.41.clone.1 | convolution fusion | flops 1105723392 | bytes 2705920 | tf_op jit(solution)/shard_map/while/body/eval_jaxpr/dot_general | solution.py:19
  60.8 0.1 fusion.67
  60.9 0.6 dynamic_slice.22
  61.5 0.6 iota_add_fusion.5
  62.1 6.6 %fusion.68 = bf16[8,512,512]{2,1,0:T(8,128)(2,1)} fusion(bf16[8,512,512]{2,1,0:T(8,128)(2,1)} %get-tuple-element.278, s32[]{:T(128)} %get-tuple-element.277, bf16[2048,512]{1,0:T(8,128)(2,1)} %get-tuple-element.287, s32[2048]{0:T(1024)S(1)} %bitcast.126, s32[2048]{0:T(1024)S(1)} %bitcast.127, s32[2048]{0:T(1024)S(1)} %bitcast.128, ...), kind=kOutput, calls=%fused_computation.41.clone.1 | convolution fusion | flops 1105723392 | bytes 2705920 | tf_op jit(solution)/shard_map/while/body/eval_jaxpr/dot_general | solution.py:19
  68.7 0.1 fusion.67
  68.8 0.6 dynamic_slice.22
  69.4 0.6 iota_add_fusion.5
  70.1 6.6 %fusion.68 = bf16[8,512,512]{2,1,0:T(8,128)(2,1)} fusion(bf16[8,512,512]{2,1,0:T(8,128)(2,1)} %get-tuple-element.278, s32[]{:T(128)} %get-tuple-element.277, bf16[2048,512]{1,0:T(8,128)(2,1)} %get-tuple-element.287, s32[2048]{0:T(1024)S(1)} %bitcast.126, s32[2048]{0:T(1024)S(1)} %bitcast.127, s32[2048]{0:T(1024)S(1)} %bitcast.128, ...), kind=kOutput, calls=%fused_computation.41.clone.1 | convolution fusion | flops 1105723392 | bytes 2705920 | tf_op jit(solution)/shard_map/while/body/eval_jaxpr/dot_general | solution.py:19
  76.7 0.0 all-reduce.4.cloned.1.call-update
  76.7 0.0 copy-start.1
  76.7 0.2 all-reduce.6.cloned.1.call-start
  77.0 4.6 fusion.41
  81.5 39.8 %while.22 = (s32[]{:T(128)}, bf16[4,512,512]{2,1,0:T(8,128)(2,1)}, s32[2048,15]{0,1:T(8,128)S(1)}, s32[4]{0:T(128)S(1)}, bf16[2048,512]{1,0:T(8,128)(2,1)}, /*index=5*/s32[]{:T(128)}) while((s32[]{:T(128)}, bf16[4,512,512]{2,1,0:T(8,128)(2,1)}, s32[2048,15]{0,1:T(8,128)S(1)}, s32[4]{0:T(128)S(1)}, bf16[2048,512]{1,0:T(8,128)(2,1)}, ...), condition=%wide.region_1.2_spmd.clone, body=%wide.region_0.1_spmd.clone.sunk | while | flops 1121452544 | bytes 2994773 | solution.py:23
  81.5 0.1 fusion.64
  81.6 0.6 dynamic_slice.21
  82.2 0.6 iota_add_fusion.4
  82.9 8.6 %fusion.65 = bf16[4,512,512]{2,1,0:T(8,128)(2,1)} fusion(bf16[4,512,512]{2,1,0:T(8,128)(2,1)} %get-tuple-element.260, s32[]{:T(128)} %get-tuple-element.259, bf16[2048,512]{1,0:T(8,128)(2,1)} %get-tuple-element.269, s32[2048]{0:T(1024)S(1)} %bitcast.111, s32[2048]{0:T(1024)S(1)} %bitcast.112, s32[2048]{0:T(1024)S(1)} %bitcast.113, ...), kind=kOutput, calls=%fused_computation.23.clone.1 | convolution fusion | flops 1121452032 | bytes 2746880 | tf_op jit(solution)/shard_map/while/body/eval_jaxpr/dot_general | solution.py:19
  91.5 0.1 fusion.64
  91.6 0.6 dynamic_slice.21
  92.2 0.6 iota_add_fusion.4
  92.9 8.6 %fusion.65 = bf16[4,512,512]{2,1,0:T(8,128)(2,1)} fusion(bf16[4,512,512]{2,1,0:T(8,128)(2,1)} %get-tuple-element.260, s32[]{:T(128)} %get-tuple-element.259, bf16[2048,512]{1,0:T(8,128)(2,1)} %get-tuple-element.269, s32[2048]{0:T(1024)S(1)} %bitcast.111, s32[2048]{0:T(1024)S(1)} %bitcast.112, s32[2048]{0:T(1024)S(1)} %bitcast.113, ...), kind=kOutput, calls=%fused_computation.23.clone.1 | convolution fusion | flops 1121452032 | bytes 2746880 | tf_op jit(solution)/shard_map/while/body/eval_jaxpr/dot_general | solution.py:19
  101.5 0.1 fusion.64
  101.5 0.6 dynamic_slice.21
  102.2 0.6 iota_add_fusion.4
  102.8 8.6 %fusion.65 = bf16[4,512,512]{2,1,0:T(8,128)(2,1)} fusion(bf16[4,512,512]{2,1,0:T(8,128)(2,1)} %get-tuple-element.260, s32[]{:T(128)} %get-tuple-element.259, bf16[2048,512]{1,0:T(8,128)(2,1)} %get-tuple-element.269, s32[2048]{0:T(1024)S(1)} %bitcast.111, s32[2048]{0:T(1024)S(1)} %bitcast.112, s32[2048]{0:T(1024)S(1)} %bitcast.113, ...), kind=kOutput, calls=%fused_computation.23.clone.1 | convolution fusion | flops 1121452032 | bytes 2746880 | tf_op jit(solution)/shard_map/while/body/eval_jaxpr/dot_general | solution.py:19
  111.4 0.1 fusion.64
  111.5 0.6 dynamic_slice.21
  112.1 0.6 iota_add_fusion.4
  112.8 8.6 %fusion.65 = bf16[4,512,512]{2,1,0:T(8,128)(2,1)} fusion(bf16[4,512,512]{2,1,0:T(8,128)(2,1)} %get-tuple-element.260, s32[]{:T(128)} %get-tuple-element.259, bf16[2048,512]{1,0:T(8,128)(2,1)} %get-tuple-element.269, s32[2048]{0:T(1024)S(1)} %bitcast.111, s32[2048]{0:T(1024)S(1)} %bitcast.112, s32[2048]{0:T(1024)S(1)} %bitcast.113, ...), kind=kOutput, calls=%fused_computation.23.clone.1 | convolution fusion | flops 1121452032 | bytes 2746880 | tf_op jit(solution)/shard_map/while/body/eval_jaxpr/dot_general | solution.py:19
  121.4 4.6 fusion.50
  126.0 66.5 %all-reduce.4.cloned.1.call-done = bf16[4096,512]{1,0:T(8,128)(2,1)} async-done(((bf16[4096,512]{1,0:T(8,128)(2,1)}), bf16[4096,512]{1,0:T(8,128)(2,1)}) %all-reduce.4.cloned.1.call-update) | async-done | bytes 4194320 | tf_op jit(solution)/shard_map/psum | solution.py:44
  192.5 3.6 add_bitcast_fusion
  196.0 0.0 all-reduce.6.cloned.1.call-update
  196.0 266.8 %all-reduce.6.cloned.1.call-done = (f32[768,512]{0,1:T(8,128)}, f32[512,512]{1,0:T(8,128)}) async-done(((f32[768,512]{0,1:T(8,128)}, f32[512,512]{1,0:T(8,128)}), (f32[768,512]{0,1:T(8,128)}, f32[512,512]{1,0:T(8,128)})) %all-reduce.6.cloned.1.call-update) | async-done | bytes 2621456 | tf_op jit(solution)/shard_map/psum | solution.py:51
  462.9 3.0 copy.10
  465.9 2.3 copy.30
  (9 shorter events, 0.0 us)
Async XLA Ops:
  7.2 114.2 %copy-start = (bf16[2048,768]{1,0:T(8,128)(2,1)S(1)}, bf16[2048,768]{1,0:T(8,128)(2,1)}, u32[]{:S(2)}) copy-start(bf16[2048,768]{1,0:T(8,128)(2,1)} %param.19) | copy-start | bytes 9437188
  7.2 185.3 %all-reduce.4.cloned.1.call-start = ((), (), s32[]{:S(2)}) async-start(), calls=%async_computation | async-start | bytes 8388608 | tf_op jit(solution)/shard_map/psum | solution.py:44
  8.1 5.2 %copy-start.2 = (s32[2048,10]{0,1:T(8,128)S(1)}, s32[2048,10]{0,1:T(8,128)}, u32[]{:S(2)}) copy-start(s32[2048,10]{0,1:T(8,128)} %param.16) | copy-start | bytes 245764
  76.7 4.8 %copy-start.1 = (s32[2048,15]{0,1:T(8,128)S(1)}, s32[2048,15]{0,1:T(8,128)}, u32[]{:S(2)}) copy-start(s32[2048,15]{0,1:T(8,128)} %param.17) | copy-start | bytes 368644
  76.7 386.1 %all-reduce.6.cloned.1.call-start = ((), (), s32[]{:S(2)}) async-start(), calls=%async_computation.1 | async-start | bytes 5242880 | tf_op jit(solution)/shard_map/psum | solution.py:51
Sparse Core Ops, SparseCore 0:
  76.8 115.5 all-reduce.3
  198.6 264.2 all-reduce.5
where the time goes:
time: 476 us; the launch traced here: 475 us
  waiting for transfers between devices  333 us (70%)
  matrix products  105 us (22%)
  between operations  14.9 us (3%)
  local copies, waits for them, and re-layouts  13.6 us (3%)
  other arithmetic  7.56 us (2%)
    psum x1, waiting for transfers between devices, on_device(): total_one, total_two = lax.psum((grad_one, grad_two), ('clique', 'copy'))  267 us
    dot_general x12, matrix products, one_block(): jnp.dot(counts.astype(jnp.bfloat16), row_grad, preferred_element_type=jnp...  87.3 us
    psum x1, waiting for transfers between devices, on_device(): summed = lax.psum(hot_part, 'clique').astype(jnp.float32)  66.5 us
  transfers between devices with their start and end apart: 2, of which 2 were waited for; matrix products, arithmetic and copies ran while one was open for 10% of the time, Pallas kernels for 0%

commit v1 on v0

--- a/solution.py
+++ b/solution.py
@@ -48,7 +48,8 @@
     grad_one = grad_one + jnp.dot(
         hot_feats.T, owned.astype(jnp.bfloat16), preferred_element_type=jnp.float32
     )
-    total_one, total_two = lax.psum((grad_one, grad_two), ("clique", "copy"))
+    heaps_touch = lambda z_in, axis_id, axis_name: lax.psum(lax.psum(z_in, axis_id), axis_name)
+    total_one, total_two = heaps_touch((grad_one, grad_two), "copy", "clique")
     return (total_one, total_two)
 
 

time: 476 us -> 548 us (1.15)
  waiting for transfers between devices: 333 us -> 403 us
    psum x1 -> x2, waiting for transfers between devices: 267 us -> 336 us  [the longest x1 234 us: on_device(): lax.psum(z_in, axis_id)]
  transfers between devices with their start and end apart: 2 -> 3, of which waited for: 2 -> 3; matrix products, arithmetic and copies ran while one was open for 10% -> 9% of each run, Pallas kernels for 0% -> 0%
where the time goes in v1:
time: 548 us; the launch traced here: 544 us
  waiting for transfers between devices  403 us (74%)
  matrix products  105 us (19%)
  between operations  14.6 us (3%)
  local copies, waits for them, and re-layouts  13.7 us (2%)
  other arithmetic  7.46 us (1%)
    psum x1, waiting for transfers between devices, on_device(): lax.psum(z_in, axis_id)  234 us
    psum x1, waiting for transfers between devices, on_device(): lax.psum(lax.psum(z_in, axis_id), axis_name)  102 us
    dot_general x12, matrix products, one_block(): jnp.dot(counts.astype(jnp.bfloat16), row_grad, preferred_element_type=jnp...  87.3 us
    psum x1, waiting for transfers between devices, on_device(): summed = lax.psum(hot_part, 'clique').astype(jnp.float32)  66.6 us
  transfers between devices with their start and end apart: 3, of which 3 were waited for; matrix products, arithmetic and copies ran while one was open for 9% of the time, Pallas kernels for 0%

profile of v1, /device:TPU:2, one launch (start us, length us, event | category | flops | bytes accessed | tf_op | source)
XLA Modules:
  0.0 544.1 jit_solution(16237619258299428963)
XLA Ops:
  7.2 0.0 all-reduce.6.cloned.1.call-start
  8.1 5.2 select_convert_fusion
  13.3 63.5 %while.23 = (s32[]{:T(128)}, bf16[8,512,512]{2,1,0:T(8,128)(2,1)}, s32[2048,10]{0,1:T(8,128)S(1)}, s32[8]{0:T(128)S(1)}, bf16[2048,512]{1,0:T(8,128)(2,1)}, /*index=5*/s32[]{:T(128)}) while((s32[]{:T(128)}, bf16[8,512,512]{2,1,0:T(8,128)(2,1)}, s32[2048,10]{0,1:T(8,128)S(1)}, s32[8]{0:T(128)S(1)}, bf16[2048,512]{1,0:T(8,128)(2,1)}, ...), condition=%wide.region_3.4_spmd.clone, body=%wide.region_2.3_spmd.clone.sunk | while | flops 1105723904 | bytes 2871893 | solution.py:23
  13.3 0.1 fusion.67
  13.3 0.7 dynamic_slice.22
  14.0 0.6 iota_add_fusion.5
  14.6 6.6 %fusion.68 = bf16[8,512,512]{2,1,0:T(8,128)(2,1)} fusion(bf16[8,512,512]{2,1,0:T(8,128)(2,1)} %get-tuple-element.280, s32[]{:T(128)} %get-tuple-element.279, bf16[2048,512]{1,0:T(8,128)(2,1)} %get-tuple-element.289, s32[2048]{0:T(1024)S(1)} %bitcast.126, s32[2048]{0:T(1024)S(1)} %bitcast.127, s32[2048]{0:T(1024)S(1)} %bitcast.128, ...), kind=kOutput, calls=%fused_computation.41.clone.1 | convolution fusion | flops 1105723392 | bytes 2705920 | tf_op jit(solution)/shard_map/while/body/eval_jaxpr/dot_general | solution.py:19
  21.2 0.1 fusion.67
  21.2 0.7 dynamic_slice.22
  21.9 0.6 iota_add_fusion.5
  22.5 6.6 %fusion.68 = bf16[8,512,512]{2,1,0:T(8,128)(2,1)} fusion(bf16[8,512,512]{2,1,0:T(8,128)(2,1)} %get-tuple-element.280, s32[]{:T(128)} %get-tuple-element.279, bf16[2048,512]{1,0:T(8,128)(2,1)} %get-tuple-element.289, s32[2048]{0:T(1024)S(1)} %bitcast.126, s32[2048]{0:T(1024)S(1)} %bitcast.127, s32[2048]{0:T(1024)S(1)} %bitcast.128, ...), kind=kOutput, calls=%fused_computation.41.clone.1 | convolution fusion | flops 1105723392 | bytes 2705920 | tf_op jit(solution)/shard_map/while/body/eval_jaxpr/dot_general | solution.py:19
  29.1 0.1 fusion.67
  29.2 0.7 dynamic_slice.22
  29.8 0.6 iota_add_fusion.5
  30.5 6.6 %fusion.68 = bf16[8,512,512]{2,1,0:T(8,128)(2,1)} fusion(bf16[8,512,512]{2,1,0:T(8,128)(2,1)} %get-tuple-element.280, s32[]{:T(128)} %get-tuple-element.279, bf16[2048,512]{1,0:T(8,128)(2,1)} %get-tuple-element.289, s32[2048]{0:T(1024)S(1)} %bitcast.126, s32[2048]{0:T(1024)S(1)} %bitcast.127, s32[2048]{0:T(1024)S(1)} %bitcast.128, ...), kind=kOutput, calls=%fused_computation.41.clone.1 | convolution fusion | flops 1105723392 | bytes 2705920 | tf_op jit(solution)/shard_map/while/body/eval_jaxpr/dot_general | solution.py:19
  37.1 0.1 fusion.67
  37.1 0.7 dynamic_slice.22
  37.8 0.6 iota_add_fusion.5
  38.4 6.6 %fusion.68 = bf16[8,512,512]{2,1,0:T(8,128)(2,1)} fusion(bf16[8,512,512]{2,1,0:T(8,128)(2,1)} %get-tuple-element.280, s32[]{:T(128)} %get-tuple-element.279, bf16[2048,512]{1,0:T(8,128)(2,1)} %get-tuple-element.289, s32[2048]{0:T(1024)S(1)} %bitcast.126, s32[2048]{0:T(1024)S(1)} %bitcast.127, s32[2048]{0:T(1024)S(1)} %bitcast.128, ...), kind=kOutput, calls=%fused_computation.41.clone.1 | convolution fusion | flops 1105723392 | bytes 2705920 | tf_op jit(solution)/shard_map/while/body/eval_jaxpr/dot_general | solution.py:19
  45.0 0.1 fusion.67
  45.0 0.7 dynamic_slice.22
  45.7 0.6 iota_add_fusion.5
  46.3 6.6 %fusion.68 = bf16[8,512,512]{2,1,0:T(8,128)(2,1)} fusion(bf16[8,512,512]{2,1,0:T(8,128)(2,1)} %get-tuple-element.280, s32[]{:T(128)} %get-tuple-element.279, bf16[2048,512]{1,0:T(8,128)(2,1)} %get-tuple-element.289, s32[2048]{0:T(1024)S(1)} %bitcast.126, s32[2048]{0:T(1024)S(1)} %bitcast.127, s32[2048]{0:T(1024)S(1)} %bitcast.128, ...), kind=kOutput, calls=%fused_computation.41.clone.1 | convolution fusion | flops 1105723392 | bytes 2705920 | tf_op jit(solution)/shard_map/while/body/eval_jaxpr/dot_general | solution.py:19
  52.9 0.1 fusion.67
  53.0 0.7 dynamic_slice.22
  53.6 0.6 iota_add_fusion.5
  54.3 6.6 %fusion.68 = bf16[8,512,512]{2,1,0:T(8,128)(2,1)} fusion(bf16[8,512,512]{2,1,0:T(8,128)(2,1)} %get-tuple-element.280, s32[]{:T(128)} %get-tuple-element.279, bf16[2048,512]{1,0:T(8,128)(2,1)} %get-tuple-element.289, s32[2048]{0:T(1024)S(1)} %bitcast.126, s32[2048]{0:T(1024)S(1)} %bitcast.127, s32[2048]{0:T(1024)S(1)} %bitcast.128, ...), kind=kOutput, calls=%fused_computation.41.clone.1 | convolution fusion | flops 1105723392 | bytes 2705920 | tf_op jit(solution)/shard_map/while/body/eval_jaxpr/dot_general | solution.py:19
  60.9 0.1 fusion.67
  60.9 0.7 dynamic_slice.22
  61.6 0.6 iota_add_fusion.5
  62.2 6.6 %fusion.68 = bf16[8,512,512]{2,1,0:T(8,128)(2,1)} fusion(bf16[8,512,512]{2,1,0:T(8,128)(2,1)} %get-tuple-element.280, s32[]{:T(128)} %get-tuple-element.279, bf16[2048,512]{1,0:T(8,128)(2,1)} %get-tuple-element.289, s32[2048]{0:T(1024)S(1)} %bitcast.126, s32[2048]{0:T(1024)S(1)} %bitcast.127, s32[2048]{0:T(1024)S(1)} %bitcast.128, ...), kind=kOutput, calls=%fused_computation.41.clone.1 | convolution fusion | flops 1105723392 | bytes 2705920 | tf_op jit(solution)/shard_map/while/body/eval_jaxpr/dot_general | solution.py:19
  68.8 0.1 fusion.67
  68.9 0.7 dynamic_slice.22
  69.5 0.6 iota_add_fusion.5
  70.1 6.6 %fusion.68 = bf16[8,512,512]{2,1,0:T(8,128)(2,1)} fusion(bf16[8,512,512]{2,1,0:T(8,128)(2,1)} %get-tuple-element.280, s32[]{:T(128)} %get-tuple-element.279, bf16[2048,512]{1,0:T(8,128)(2,1)} %get-tuple-element.289, s32[2048]{0:T(1024)S(1)} %bitcast.126, s32[2048]{0:T(1024)S(1)} %bitcast.127, s32[2048]{0:T(1024)S(1)} %bitcast.128, ...), kind=kOutput, calls=%fused_computation.41.clone.1 | convolution fusion | flops 1105723392 | bytes 2705920 | tf_op jit(solution)/shard_map/while/body/eval_jaxpr/dot_general | solution.py:19
  76.8 0.0 all-reduce.6.cloned.1.call-update
  76.8 0.2 all-reduce.8.cloned.1.call-start
  77.1 4.5 fusion.41
  81.6 39.7 %while.22 = (s32[]{:T(128)}, bf16[4,512,512]{2,1,0:T(8,128)(2,1)}, s32[2048,15]{0,1:T(8,128)S(1)}, s32[4]{0:T(128)S(1)}, bf16[2048,512]{1,0:T(8,128)(2,1)}, /*index=5*/s32[]{:T(128)}) while((s32[]{:T(128)}, bf16[4,512,512]{2,1,0:T(8,128)(2,1)}, s32[2048,15]{0,1:T(8,128)S(1)}, s32[4]{0:T(128)S(1)}, bf16[2048,512]{1,0:T(8,128)(2,1)}, ...), condition=%wide.region_1.2_spmd.clone, body=%wide.region_0.1_spmd.clone.sunk | while | flops 1121452544 | bytes 2994773 | solution.py:23
  81.6 0.1 fusion.64
  81.7 0.6 dynamic_slice.21
  82.3 0.6 iota_add_fusion.4
  82.9 8.6 %fusion.65 = bf16[4,512,512]{2,1,0:T(8,128)(2,1)} fusion(bf16[4,512,512]{2,1,0:T(8,128)(2,1)} %get-tuple-element.262, s32[]{:T(128)} %get-tuple-element.261, bf16[2048,512]{1,0:T(8,128)(2,1)} %get-tuple-element.271, s32[2048]{0:T(1024)S(1)} %bitcast.111, s32[2048]{0:T(1024)S(1)} %bitcast.112, s32[2048]{0:T(1024)S(1)} %bitcast.113, ...), kind=kOutput, calls=%fused_computation.23.clone.1 | convolution fusion | flops 1121452032 | bytes 2746880 | tf_op jit(solution)/shard_map/while/body/eval_jaxpr/dot_general | solution.py:19
  91.5 0.1 fusion.64
  91.6 0.6 dynamic_slice.21
  92.2 0.6 iota_add_fusion.4
  92.8 8.6 %fusion.65 = bf16[4,512,512]{2,1,0:T(8,128)(2,1)} fusion(bf16[4,512,512]{2,1,0:T(8,128)(2,1)} %get-tuple-element.262, s32[]{:T(128)} %get-tuple-element.261, bf16[2048,512]{1,0:T(8,128)(2,1)} %get-tuple-element.271, s32[2048]{0:T(1024)S(1)} %bitcast.111, s32[2048]{0:T(1024)S(1)} %bitcast.112, s32[2048]{0:T(1024)S(1)} %bitcast.113, ...), kind=kOutput, calls=%fused_computation.23.clone.1 | convolution fusion | flops 1121452032 | bytes 2746880 | tf_op jit(solution)/shard_map/while/body/eval_jaxpr/dot_general | solution.py:19
  101.4 0.1 fusion.64
  101.5 0.6 dynamic_slice.21
  102.1 0.6 iota_add_fusion.4
  102.8 8.6 %fusion.65 = bf16[4,512,512]{2,1,0:T(8,128)(2,1)} fusion(bf16[4,512,512]{2,1,0:T(8,128)(2,1)} %get-tuple-element.262, s32[]{:T(128)} %get-tuple-element.261, bf16[2048,512]{1,0:T(8,128)(2,1)} %get-tuple-element.271, s32[2048]{0:T(1024)S(1)} %bitcast.111, s32[2048]{0:T(1024)S(1)} %bitcast.112, s32[2048]{0:T(1024)S(1)} %bitcast.113, ...), kind=kOutput, calls=%fused_computation.23.clone.1 | convolution fusion | flops 1121452032 | bytes 2746880 | tf_op jit(solution)/shard_map/while/body/eval_jaxpr/dot_general | solution.py:19
  111.4 0.1 fusion.64
  111.5 0.6 dynamic_slice.21
  112.1 0.6 iota_add_fusion.4
  112.7 8.6 %fusion.65 = bf16[4,512,512]{2,1,0:T(8,128)(2,1)} fusion(bf16[4,512,512]{2,1,0:T(8,128)(2,1)} %get-tuple-element.262, s32[]{:T(128)} %get-tuple-element.261, bf16[2048,512]{1,0:T(8,128)(2,1)} %get-tuple-element.271, s32[2048]{0:T(1024)S(1)} %bitcast.111, s32[2048]{0:T(1024)S(1)} %bitcast.112, s32[2048]{0:T(1024)S(1)} %bitcast.113, ...), kind=kOutput, calls=%fused_computation.23.clone.1 | convolution fusion | flops 1121452032 | bytes 2746880 | tf_op jit(solution)/shard_map/while/body/eval_jaxpr/dot_general | solution.py:19
  121.3 4.6 fusion.50
  125.9 66.6 %all-reduce.6.cloned.1.call-done = bf16[4096,512]{1,0:T(8,128)(2,1)} async-done(((bf16[4096,512]{1,0:T(8,128)(2,1)}), bf16[4096,512]{1,0:T(8,128)(2,1)}) %all-reduce.6.cloned.1.call-update) | async-done | bytes 4194320 | tf_op jit(solution)/shard_map/psum | solution.py:44
  192.6 3.6 add_bitcast_fusion
  196.1 0.0 all-reduce.8.cloned.1.call-update
  196.2 0.0 all-reduce.10.cloned.1.call-start
  196.2 234.1 %all-reduce.8.cloned.1.call-done = (f32[768,512]{0,1:T(8,128)}, f32[512,512]{1,0:T(8,128)}) async-done(((f32[768,512]{0,1:T(8,128)}, f32[512,512]{1,0:T(8,128)}), (f32[768,512]{0,1:T(8,128)}, f32[512,512]{1,0:T(8,128)})) %all-reduce.8.cloned.1.call-update) | async-done | bytes 2621456 | tf_op jit(solution)/shard_map/psum | solution.py:51
  430.3 102.0 %all-reduce.10.cloned.1.call-done = (f32[768,512]{0,1:T(8,128)}, f32[512,512]{1,0:T(8,128)}) async-done(((f32[768,512]{0,1:T(8,128)}, f32[512,512]{1,0:T(8,128)}), (f32[768,512]{0,1:T(8,128)}, f32[512,512]{1,0:T(8,128)})) %all-reduce.10.cloned.1.call-update) | async-done | bytes 2621456 | tf_op jit(solution)/shard_map/psum | solution.py:51
  532.3 3.0 copy.10
  535.4 2.3 copy.32
  (12 shorter events, 0.1 us)
Async XLA Ops:
  7.2 114.2 %copy-start = (bf16[2048,768]{1,0:T(8,128)(2,1)S(1)}, bf16[2048,768]{1,0:T(8,128)(2,1)}, u32[]{:S(2)}) copy-start(bf16[2048,768]{1,0:T(8,128)(2,1)} %param.19) | copy-start | bytes 9437188
  7.2 185.4 %all-reduce.6.cloned.1.call-start = ((), (), s32[]{:S(2)}) async-start(), calls=%async_computation | async-start | bytes 8388608 | tf_op jit(solution)/shard_map/psum | solution.py:44
  8.1 5.2 copy-start.2
  76.8 4.8 copy-start.1
  76.8 353.5 %all-reduce.8.cloned.1.call-start = ((), (), s32[]{:S(2)}) async-start(), calls=%async_computation.1 | async-start | bytes 5242880 | tf_op jit(solution)/shard_map/psum | solution.py:51
  196.2 336.2 %all-reduce.10.cloned.1.call-start = ((), (), s32[]{:S(2)}) async-start(), calls=%async_computation.2 | async-start | bytes 5242880 | tf_op jit(solution)/shard_map/psum | solution.py:51
Sparse Core Ops, SparseCore 0:
  76.9 115.6 all-reduce.5
  196.3 233.9 all-reduce.7
  433.0 99.2 all-reduce.9
